TPU v7x, 32 devices: a whole 2x2x4 slice. The times are simulated.
32 devices in a mesh: dp: 4 (over x, core), row: 4 (over z), col: 2 (over y).
Axes of the slice: x: 2, y: 2, z: 4, core: 2. Of those that a mesh axis runs over, the one named last changes fastest.
Arguments:
- tokens_in: bfloat16 [8192, 768], P(('dp', 'col'), 'row'), may hold values from -6 to 6
- out_cot: bfloat16 [8192, 768], P(('dp', 'col'), 'row'), may hold values from -6 to 6
- segments: int32 [16, 512], P('dp'), may hold values from 0 to 31, never falling along the last dimension, each value on 1 to 256 neighbouring positions
- norm_params: float32 [4, 768], P(None, 'row'), may hold values from -1.2 to 1.5, as said below
- qkv_weight: float32 [768, 2304], P('row', 'col'), may hold values from -0.21875 to 0.21875
- proj_weight: float32 [768, 768], P('col', 'row'), may hold values from -0.875 to 0.875
- up_weight: float32 [768, 3072], P('row', 'col'), may hold values from -0.21875 to 0.21875
- down_weight: float32 [3072, 768], P('col', 'row'), may hold values from -0.109375 to 0.109375
- norm_first: float32 [4, 768], P(None, 'row'), may hold values from -18 to 18
- norm_second: float32 [4, 768], P(None, 'row'), may hold values from 30 to 300
- qkv_first: float32 [768, 2304], P('row', 'col'), may hold values from -18 to 18
- qkv_second: float32 [768, 2304], P('row', 'col'), may hold values from 30 to 300
- proj_first: float32 [768, 768], P('col', 'row'), may hold values from -18 to 18
- proj_second: float32 [768, 768], P('col', 'row'), may hold values from 30 to 300
- up_first: float32 [768, 3072], P('row', 'col'), may hold values from -18 to 18
- up_second: float32 [768, 3072], P('row', 'col'), may hold values from 30 to 300
- down_first: float32 [3072, 768], P('col', 'row'), may hold values from -18 to 18
- down_second: float32 [3072, 768], P('col', 'row'), may hold values from 30 to 300
Outputs:
- output: bfloat16 [8192, 768], P(('dp', 'col'), 'row')
- input_grad: bfloat16 [8192, 768], P(('dp', 'col'), 'row')
- norm_grad: float32 [4, 768], P(None, 'row')
- qkv_grad: float32 [768, 2304], P('row', 'col')
- proj_grad: float32 [768, 768], P('col', 'row')
- up_grad: float32 [768, 3072], P('row', 'col')
- down_grad: float32 [3072, 768], P('col', 'row')
- norm_new: float32 [4, 768], P(None, 'row')
- qkv_new: float32 [768, 2304], P('row', 'col')
- proj_new: float32 [768, 768], P('col', 'row')
- up_new: float32 [768, 3072], P('row', 'col')
- down_new: float32 [3072, 768], P('col', 'row')
- norm_first_new: float32 [4, 768], P(None, 'row')
- norm_second_new: float32 [4, 768], P(None, 'row')
- qkv_first_new: float32 [768, 2304], P('row', 'col')
- qkv_second_new: float32 [768, 2304], P('row', 'col')
- proj_first_new: float32 [768, 768], P('col', 'row')
- proj_second_new: float32 [768, 768], P('col', 'row')
- up_first_new: float32 [768, 3072], P('row', 'col')
- up_second_new: float32 [768, 3072], P('row', 'col')
- down_first_new: float32 [3072, 768], P('col', 'row')
- down_second_new: float32 [3072, 768], P('col', 'row')
Inputs may be any that keep to these rules, and one draw needn't show every extreme that they name: `segments`: within a row the numbers never fall; no number covers more than 256 positions of a row, and one covers exactly that many. `norm_params`: rows 0 and 2 lie in 0.5 to 1.5.
All inputs are finite; a program needn't handle non-finite values.
Results may differ from a plain program's by a relative error of at most 0.0093.
Values may be sent and summed in bfloat16 or wider, within the bound.
A program may use at most 192 MiB of HBM per device.

v0:
```python
import math
import jax
import jax.numpy as jnp
from jax import lax
from jax.sharding import PartitionSpec as P

D = 768
HEAD_DIM = 64
ROT_DIM = 16
SEQ_LEN = 512
STEP = 3
norm_eps = 1e-05
rotary_base = 10000.0
learn_rate = 0.01
beta_first = 0.9
beta_second = 0.95
adam_eps = 1e-08
decay_rate = 0.1
mask_fill = -1e30
inv_sqrt_two = 0.7071067811865476
inv_sqrt_two_pi = 0.3989422804014327


def gelu_value(value):
    return 0.5 * value * (1.0 + lax.erf(value * inv_sqrt_two))


def gelu_slope(value):
    return 0.5 * (1.0 + lax.erf(value * inv_sqrt_two)) + value * inv_sqrt_two_pi * jnp.exp(
        -0.5 * value * value
    )


def positions_of(segs):
    length = segs.shape[-1]
    index = jnp.broadcast_to(jnp.arange(length, dtype=jnp.int32), segs.shape)
    starts = jnp.concatenate(
        [jnp.ones(segs.shape[:-1] + (1,), bool), segs[..., 1:] != segs[..., :-1]], -1
    )
    first = lax.cummax(jnp.where(starts, index, 0), axis=segs.ndim - 1)
    return index - first


def rotary_tables(positions):
    half = ROT_DIM // 2
    freq = rotary_base ** (-2.0 * jnp.arange(half, dtype=jnp.float32) / ROT_DIM)
    angle = positions.astype(jnp.float32)[..., None] * freq
    return (jnp.cos(angle), jnp.sin(angle))


def rotate(tensor, cosine, sine):
    half = ROT_DIM // 2
    cos_part = cosine[..., None, :]
    sin_part = sine[..., None, :]
    front = tensor[..., :half]
    back = tensor[..., half:ROT_DIM]
    return jnp.concatenate(
        [
            front * cos_part - back * sin_part,
            back * cos_part + front * sin_part,
            tensor[..., ROT_DIM:],
        ],
        -1,
    )


def rotate_back(grad, cosine, sine):
    half = ROT_DIM // 2
    cos_part = cosine[..., None, :]
    sin_part = sine[..., None, :]
    front = grad[..., :half]
    back = grad[..., half:ROT_DIM]
    return jnp.concatenate(
        [
            front * cos_part + back * sin_part,
            back * cos_part - front * sin_part,
            grad[..., ROT_DIM:],
        ],
        -1,
    )


def masked_scores(query, keys, segment):
    length = segment.shape[0]
    scores = jnp.einsum(
        "qhd,khd->hqk", query, keys, preferred_element_type=jnp.float32
    ) / math.sqrt(HEAD_DIM)
    index = jnp.arange(length, dtype=jnp.int32)
    allowed = (segment[:, None] == segment[None, :]) & (index[None, :] <= index[:, None])
    return jnp.where(allowed[None], scores, mask_fill)


def attend(query, keys, values, segment):
    scores = masked_scores(query, keys, segment)
    total = jnp.sum(jnp.exp(scores), -1, keepdims=True)
    logsum = jnp.log(total)
    weights = jnp.exp(scores - logsum).astype(jnp.bfloat16)
    mixed = jnp.einsum("hqk,khd->qhd", weights, values, preferred_element_type=jnp.float32).astype(
        jnp.bfloat16
    )
    return (mixed, logsum[..., 0])


def attend_back(query, keys, values, segment, logsum, mixed, grad_mixed):
    scores = masked_scores(query, keys, segment)
    probs = jnp.exp(scores - logsum[..., None])
    weights = probs.astype(jnp.bfloat16)
    value_grad = jnp.einsum("hqk,qhd->khd", weights, grad_mixed, preferred_element_type=jnp.float32)
    prod_grad = jnp.einsum("qhd,khd->hqk", grad_mixed, values, preferred_element_type=jnp.float32)
    delta = jnp.sum(grad_mixed.astype(jnp.float32) * mixed.astype(jnp.float32), -1).T
    score_grad = (probs * (prod_grad - delta[..., None]) / math.sqrt(HEAD_DIM)).astype(jnp.bfloat16)
    query_grad = jnp.einsum("hqk,khd->qhd", score_grad, keys, preferred_element_type=jnp.float32)
    key_grad = jnp.einsum("hqk,qhd->khd", score_grad, query, preferred_element_type=jnp.float32)
    return (query_grad, key_grad, value_grad)


def dot32(left, right):
    return jnp.dot(left, right, preferred_element_type=jnp.float32)


def dot_rows(left, right):
    return lax.dot_general(
        left, right, (((0,), (0,)), ((), ())), preferred_element_type=jnp.float32
    )


def dot_cols(left, right):
    return lax.dot_general(
        left, right, (((1,), (1,)), ((), ())), preferred_element_type=jnp.float32
    )


def adam_update(weight, first, second, grad, decay):
    first_new = beta_first * first + (1.0 - beta_first) * grad
    second_new = beta_second * second + (1.0 - beta_second) * grad * grad
    first_hat = first_new / (1.0 - beta_first**STEP)
    second_hat = second_new / (1.0 - beta_second**STEP)
    weight_new = weight - learn_rate * (
        first_hat / (jnp.sqrt(second_hat) + adam_eps) + decay * weight
    )
    return (weight_new, first_new, second_new)


def gather_weight(piece):
    rows = piece.shape[0] // lax.axis_size("dp")
    own = lax.dynamic_slice_in_dim(piece, lax.axis_index("dp") * rows, rows, 0)
    return lax.all_gather(own, ("row", "dp"), axis=0, tiled=True)


def reduce_weights(grads):
    whole = jnp.concatenate([grad.astype(jnp.bfloat16) for grad in grads], 1)
    part = lax.psum_scatter(whole, ("row", "dp"), scatter_dimension=0, tiled=True)
    sums, start = ([], 0)
    for grad in grads:
        piece = part[:, start : start + grad.shape[1]]
        sums.append(lax.all_gather(piece, "dp", axis=0, tiled=True).astype(jnp.float32))
        start += grad.shape[1]
    return sums


def on_device(
    tokens_in,
    out_cot,
    segments,
    norm_params,
    qkv_weight,
    proj_weight,
    up_weight,
    down_weight,
    norm_first,
    norm_second,
    qkv_first,
    qkv_second,
    proj_first,
    proj_second,
    up_first,
    up_second,
    down_first,
    down_second,
):
    row_count = lax.axis_size("row")
    row_index = lax.axis_index("row")
    col_count = lax.axis_size("col")
    col_index = lax.axis_index("col")
    local_count, local_width = tokens_in.shape
    heads_here = qkv_weight.shape[1] // (3 * HEAD_DIM)
    seq_count = segments.shape[0] // row_count
    group_count = local_count * col_count
    share = group_count // row_count
    width = local_width * row_count
    bf16 = jnp.bfloat16

    def to_tokens(rows):
        blocks = rows.reshape(row_count, share, local_width)
        blocks = lax.all_to_all(blocks, "row", 0, 0, tiled=True)
        return jnp.moveaxis(blocks, 0, 1).reshape(share, width)

    x16 = to_tokens(lax.all_gather(tokens_in, "col", axis=0, tiled=True))
    cot16 = to_tokens(lax.all_gather(out_cot, "col", axis=0, tiled=True))
    norm_full = lax.all_gather(norm_params, "row", axis=1, tiled=True)
    pieces = (qkv_weight, up_weight, proj_weight.T, down_weight.T)
    all16 = gather_weight(jnp.concatenate([piece.astype(bf16) for piece in pieces], 1))
    first_cut = qkv_weight.shape[1]
    second_cut = first_cut + up_weight.shape[1]
    qkv16 = all16[:, :first_cut]
    up16 = all16[:, first_cut:second_cut]
    out16 = all16[:, second_cut:]
    xfull = x16.astype(jnp.float32)
    mean = jnp.sum(xfull, 1, keepdims=True) / D
    spread = jnp.sum(xfull * xfull, 1, keepdims=True) / D - mean * mean
    rstd = lax.rsqrt(spread + norm_eps)
    normed = (xfull - mean) * rstd
    first_in = (normed * norm_full[0] + norm_full[1]).astype(bf16)
    second_in = (normed * norm_full[2] + norm_full[3]).astype(bf16)
    qkv_own = dot32(first_in, qkv16)
    hidden_here = dot32(second_in, up16)
    width_qkv = qkv16.shape[1]
    seg_own = lax.dynamic_slice_in_dim(segments, row_index * seq_count, seq_count, 0)
    cosine, sine = rotary_tables(positions_of(seg_own))
    packed = qkv_own.reshape(seq_count, SEQ_LEN, heads_here, 3, HEAD_DIM)
    query = rotate(packed[..., 0, :], cosine, sine).astype(bf16)
    keys = rotate(packed[..., 1, :], cosine, sine).astype(bf16)
    values = packed[..., 2, :].astype(bf16)
    attended, logsum = lax.map(lambda item: attend(*item), (query, keys, values, seg_own))
    attn_width = heads_here * HEAD_DIM
    attn_flat = attended.reshape(share, attn_width)
    active = gelu_value(hidden_here).astype(bf16)
    act_cat = jnp.concatenate([attn_flat, active], 1)
    out_part = dot_cols(act_cat, out16)
    out_grad = dot_rows(cot16, act_cat)
    act_grad = dot32(cot16, out16)
    attended_grad = act_grad[:, :attn_width].astype(bf16)
    hidden_grad = (act_grad[:, attn_width:] * gelu_slope(hidden_here)).astype(bf16)
    up_grad = dot_rows(second_in, hidden_grad)
    grad_heads = attended_grad.reshape(seq_count, SEQ_LEN, heads_here, HEAD_DIM)
    query_grad, key_grad, value_grad = lax.map(
        lambda item: attend_back(*item),
        (query, keys, values, seg_own, logsum, attended, grad_heads),
    )
    query_grad = rotate_back(query_grad, cosine, sine)
    key_grad = rotate_back(key_grad, cosine, sine)
    packed_grad = (
        jnp.stack([query_grad, key_grad, value_grad], 3).reshape(share, width_qkv).astype(bf16)
    )
    qkv_grad = dot_rows(first_in, packed_grad)
    qkv_grad, up_grad, out_grad = reduce_weights((qkv_grad, up_grad, out_grad))
    first_grad = dot_cols(packed_grad, qkv16)
    second_grad = dot_cols(hidden_grad, up16)
    norm_part = jnp.stack(
        [
            jnp.sum(first_grad * normed, 0),
            jnp.sum(first_grad, 0),
            jnp.sum(second_grad * normed, 0),
            jnp.sum(second_grad, 0),
        ],
        0,
    )
    combined = norm_full[0] * first_grad + norm_full[2] * second_grad
    back_first = jnp.sum(combined, 1, keepdims=True) / D
    back_second = jnp.sum(combined * normed, 1, keepdims=True) / D
    grad_part = rstd * (combined - back_first - normed * back_second)

    def to_features(part):
        blocks = part.astype(bf16).reshape(share, row_count, local_width)
        blocks = lax.all_to_all(jnp.moveaxis(blocks, 1, 0), "row", 0, 0, tiled=True)
        parts = blocks.reshape(col_count, local_count, local_width)
        total = lax.dynamic_index_in_dim(parts, col_index, 0, keepdims=False).astype(jnp.float32)
        for step in range(1, col_count):
            peer = lax.rem(col_index + step, col_count)
            sent = lax.dynamic_index_in_dim(parts, peer, 0, keepdims=False)
            ring = [(i, (i + step) % col_count) for i in range(col_count)]
            total = total + lax.ppermute(sent, "col", ring).astype(jnp.float32)
        return total

    output = (tokens_in.astype(jnp.float32) + to_features(out_part)).astype(bf16)
    input_grad = (out_cot.astype(jnp.float32) + to_features(grad_part)).astype(bf16)
    norm_grad = lax.dynamic_slice_in_dim(
        lax.psum(norm_part, ("dp", "row", "col")), row_index * local_width, local_width, 1
    )
    proj_grad = out_grad[:, :attn_width].T
    down_grad = out_grad[:, attn_width:].T
    norm_new, norm_first_new, norm_second_new = adam_update(
        norm_params, norm_first, norm_second, norm_grad, 0.0
    )
    qkv_new, qkv_first_new, qkv_second_new = adam_update(
        qkv_weight, qkv_first, qkv_second, qkv_grad, decay_rate
    )
    proj_new, proj_first_new, proj_second_new = adam_update(
        proj_weight, proj_first, proj_second, proj_grad, decay_rate
    )
    up_new, up_first_new, up_second_new = adam_update(
        up_weight, up_first, up_second, up_grad, decay_rate
    )
    down_new, down_first_new, down_second_new = adam_update(
        down_weight, down_first, down_second, down_grad, decay_rate
    )
    return (
        output,
        input_grad,
        norm_grad,
        qkv_grad,
        proj_grad,
        up_grad,
        down_grad,
        norm_new,
        qkv_new,
        proj_new,
        up_new,
        down_new,
        norm_first_new,
        norm_second_new,
        qkv_first_new,
        qkv_second_new,
        proj_first_new,
        proj_second_new,
        up_first_new,
        up_second_new,
        down_first_new,
        down_second_new,
    )


def solution(mesh):
    placed = (
        P(("dp", "col"), "row"),
        P(("dp", "col"), "row"),
        P("dp", None),
        P(None, "row"),
        P("row", "col"),
        P("col", "row"),
        P("row", "col"),
        P("col", "row"),
        P(None, "row"),
        P(None, "row"),
        P("row", "col"),
        P("row", "col"),
        P("col", "row"),
        P("col", "row"),
        P("row", "col"),
        P("row", "col"),
        P("col", "row"),
        P("col", "row"),
    )
    return jax.shard_map(
        on_device,
        mesh=mesh,
        in_specs=placed,
        out_specs=(
            P(("dp", "col"), "row"),
            P(("dp", "col"), "row"),
            P(None, "row"),
            P("row", "col"),
            P("col", "row"),
            P("row", "col"),
            P("col", "row"),
            P(None, "row"),
            P("row", "col"),
            P("col", "row"),
            P("row", "col"),
            P("col", "row"),
            P(None, "row"),
            P(None, "row"),
            P("row", "col"),
            P("row", "col"),
            P("col", "row"),
            P("col", "row"),
            P("row", "col"),
            P("row", "col"),
            P("col", "row"),
            P("col", "row"),
        ),
        check_vma=False,
    )
```

profile of v0, /device:TPU:0, one launch (start us, length us, event | category | flops | bytes accessed | tf_op | source)
XLA Modules:
  0.0 313.0 jit_solution(11491301340539677173)
XLA Ops:
  10.9 12.8 %all_gather.21 = bf16[2048,192]{0,1:T(8,128)(2,1)S(1)} all-gather(bf16[1024,192]{0,1:T(8,128)(2,1)S(1)} %copy-done.13), channel_id=1, replica_groups=mesh['dp'=4,'row'=4,'col'=2] {'col'}, dimensions={0}, use_global_device_ids=true | all-gather | bytes 1179648 | tf_op jit(solution)/shard_map/all_gather | solution.py:198
  24.7 5.1 %all-to-all-start = ((bf16[4,512,192]{1,2,0:T(8,128)(2,1)}), bf16[4,512,192]{1,2,0:T(8,128)(2,1)S(1)}, u32[]{:S(2)}, u32[]{:S(2)}) async-start(bf16[4,512,192]{1,2,0:T(8,128)(2,1)} %bitcast.147), calls=%async_computation | async-start | bytes 1572864 | tf_op jit(solution)/shard_map/all_to_all | solution.py:195
  29.8 40.2 %all-gather = f32[4,192,4]{1,2,0:T(4,128)S(1)} all-gather(f32[1,192,4]{1,2,0:T(4,128)S(1)} %bitcast.167), channel_id=1, replica_groups=mesh['dp'=4,'row'=4,'col'=2] {'row'}, dimensions={0}, use_global_device_ids=true | all-gather | bytes 15360 | tf_op jit(solution)/shard_map/all_gather | solution.py:200
  71.1 8.4 %all_gather.24 = bf16[2048,192]{0,1:T(8,128)(2,1)S(1)} all-gather(bf16[1024,192]{0,1:T(8,128)(2,1)S(1)} %copy-done.11), channel_id=1, replica_groups=mesh['dp'=4,'row'=4,'col'=2] {'col'}, dimensions={0}, use_global_device_ids=true | all-gather | bytes 1179648 | tf_op jit(solution)/shard_map/all_gather | solution.py:199
  82.8 4.2 %all-to-all-start.2 = ((bf16[4,512,192]{1,2,0:T(8,128)(2,1)}), bf16[4,512,192]{1,2,0:T(8,128)(2,1)}, u32[]{:S(2)}, u32[]{:S(2)}) async-start(bf16[4,512,192]{1,2,0:T(8,128)(2,1)} %bitcast.146), calls=%async_computation.2 | async-start | bytes 1572864 | tf_op jit(solution)/shard_map/all_to_all | solution.py:195
  99.0 4.2 %all-to-all-done.2 = bf16[4,512,192]{1,2,0:T(8,128)(2,1)} async-done(((bf16[4,512,192]{1,2,0:T(8,128)(2,1)}), bf16[4,512,192]{1,2,0:T(8,128)(2,1)}, u32[]{:S(2)}, u32[]{:S(2)}) %all-to-all-start.2) | async-done | bytes 786464 | tf_op jit(solution)/shard_map/all_to_all | solution.py:195
  103.2 3.9 %convolution_bitcast_fusion = f32[512,1920]{1,0:T(8,128)S(1)} fusion(bf16[512,768]{0,1:T(8,128)(2,1)} %bitcast.31, bf16[768,4608]{1,0:T(8,128)(2,1)} %all-gather.3.cloned.1.call-done), kind=kOutput, calls=%fused_computation.12 | convolution fusion | flops 1509949440 | bytes 7667712 | tf_op jit(solution)/shard_map/dot_general | solution.py:118
  109.8 7.4 %fusion.1 = f32[6,512,512]{1,2,0:T(8,128)} fusion(pred[512,512]{0,1:T(8,128)(4,1)} %fusion.38, bf16[512,6,48]{0,2,1:T(8,128)(2,1)S(1)} %get-tuple-element.202, bf16[512,6,8]{0,2,1:T(8,128)(2,1)S(1)} %get-tuple-element.193, bf16[512,6,8]{0,2,1:T(8,128)(2,1)S(1)} %get-tuple-element.194, bf16[512,6,48]{0,2,1:T(8,128)(2,1)S(1)} %get-tuple-element.201, ...), kind=kOutput, calls=%fused_computation.3 | convolution fusion | flops 415239680 | bytes 7340032 | tf_op jit(solution)/shard_map/while/body/eval_jaxpr/reduce_sum | solution.py:95
  117.2 4.3 %multiply_reduce_fusion.4 = (f32[512,6]{0,1:T(8,128)S(1)}, bf16[6,64,512]{2,1,0:T(8,128)(2,1)}) fusion(bf16[512,6,64]{0,2,1:T(8,128)(2,1)S(1)} %bitcast.152, f32[6,512,512]{1,2,0:T(8,128)} %fusion.1, f32[1,512,6,3,64]{1,4,3,2,0:T(8,128)S(1)} %copy-done.8), kind=kOutput, calls=%fused_computation.92 | convolution fusion | flops 203879424 | bytes 7483392 | tf_op jit(solution)/shard_map/while/body/eval_jaxpr/hqk,khd->qhd/dot_general | solution.py:98
  132.3 5.9 %fusion.9 = (bf16[512,1536]{1,0:T(8,128)(2,1)S(1)}, bf16[512,1536]{1,0:T(8,128)(2,1)}) fusion(f32[512,1920]{1,0:T(8,128)} %copy-done.30, bf16[768,4608]{1,0:T(8,128)(2,1)} %all-gather.3.cloned.1.call-done, f32[512,768]{1,0:T(8,128)S(1)} %copy-done.2, f32[768]{0:T(1024)S(1)} %copy-done.41, f32[768]{0:T(1024)S(1)} %copy-done.40, f32[512]{0:T(512)S(1)} %copy-done.34, ...), kind=kOutput, calls=%fused_computation.17 | convolution fusion | flops 1220149248 | bytes 10233856 | tf_op jit(solution)/shard_map/dot_general | solution.py:118
  145.4 3.5 %fusion.13 = bf16[768,1920]{0,1:T(8,128)(2,1)S(1)} fusion(bf16[512,768]{0,1:T(8,128)(2,1)} %bitcast.31, bf16[512,1536]{1,0:T(8,128)(2,1)} %get-tuple-element.176, bf16[512,384]{1,0:T(8,128)(2,1)S(1)} %copy.202), kind=kOutput, calls=%fused_computation.23 | convolution fusion | flops 1515356160 | bytes 5701632 | tf_op jit(solution)/shard_map/dot_general | solution.py:122
  148.9 3.4 %pad_maximum_fusion = bf16[768,4608]{0,1:T(8,128)(2,1)} fusion(bf16[768,1920]{0,1:T(8,128)(2,1)S(1)} %fusion.13, bf16[768,1536]{0,1:T(8,128)(2,1)S(1)} %copy.216, bf16[768,1152]{0,1:T(8,128)(2,1)S(1)} %copy-done.1), kind=kLoop, calls=%fused_computation.1 | loop fusion | flops 21233664 | bytes 14155776 | tf_op jit(solution)/shard_map/concatenate | solution.py:151
  152.3 10.3 %copy.228 = bf16[768,4608]{1,0:T(8,128)(2,1)} copy(bf16[768,4608]{0,1:T(8,128)(2,1)} %pad_maximum_fusion) | data formatting | bytes 14155776
  164.0 3.2 %fusion.17 = f32[512,768]{1,0:T(8,128)S(1)} fusion(bf16[512,1536]{1,0:T(8,128)(2,1)S(1)} %copy-done.45, bf16[768,4608]{1,0:T(8,128)(2,1)} %all-gather.3.cloned.1.call-done), kind=kOutput, calls=%fused_computation.28 | convolution fusion | flops 1207959552 | bytes 5505024 | tf_op jit(solution)/shard_map/dot_general | solution.py:128
  167.3 3.5 %multiply_reduce_fusion.1 = (f32[768]{0:T(1024)S(1)}, f32[512]{0:T(512)S(1)}, f32[768]{0:T(1024)S(1)}, f32[768]{0:T(1024)S(1)}, f32[512]{0:T(512)S(1)}, /*index=5*/f32[768]{0:T(1024)S(1)}, f32[512,768]{1,0:T(8,128)S(1)}) fusion(f32[512,768]{1,0:T(8,128)S(1)} %copy-done.3, f32[512]{0:T(512)S(1)} %copy-done.34, f32[512]{0:T(512)S(1)} %copy-done.32, ...), kind=kOutput, calls=%fused_computation.42 | convolution fusion | flops 911470592 | bytes 7694336 | tf_op jit(solution)/shard_map/dot_general | solution.py:128
  172.4 3.5 %all-to-all-start.3 = ((bf16[4,512,192]{1,2,0:T(8,128)(2,1)}), bf16[4,512,192]{1,2,0:T(8,128)(2,1)S(1)}, u32[]{:S(2)}, u32[]{:S(2)}) async-start(bf16[4,512,192]{1,2,0:T(8,128)(2,1)} %bitcast.47), calls=%async_computation.3 | async-start | bytes 1572864 | tf_op jit(solution)/shard_map/all_to_all | solution.py:265
  175.9 4.5 %fusion.27 = bf16[512,768]{1,0:T(8,128)(2,1)S(1)} fusion(bf16[768,4608]{1,0:T(8,128)(2,1)} %all-gather.3.cloned.1.call-done, bf16[512,1536]{1,0:T(8,128)(2,1)} %get-tuple-element.176, bf16[512,384]{1,0:T(8,128)(2,1)S(1)} %copy.202), kind=kOutput, calls=%fused_computation.57 | convolution fusion | flops 1514274816 | bytes 5701632 | tf_op jit(solution)/shard_map/dot_general | solution.py:128
  181.6 11.4 %all-to-all-done.3 = bf16[4,512,192]{1,2,0:T(8,128)(2,1)S(1)} async-done(((bf16[4,512,192]{1,2,0:T(8,128)(2,1)}), bf16[4,512,192]{1,2,0:T(8,128)(2,1)S(1)}, u32[]{:S(2)}, u32[]{:S(2)}) %all-to-all-start.3) | async-done | bytes 786464 | tf_op jit(solution)/shard_map/all_to_all | solution.py:265
  193.0 3.7 %all-to-all-start.1 = ((bf16[4,512,192]{1,2,0:T(8,128)(2,1)}), bf16[4,512,192]{1,2,0:T(8,128)(2,1)S(1)}, u32[]{:S(2)}, u32[]{:S(2)}) async-start(bf16[4,512,192]{1,2,0:T(8,128)(2,1)} %bitcast.29), calls=%async_computation.1 | async-start | bytes 1572864 | tf_op jit(solution)/shard_map/all_to_all | solution.py:265
  201.5 57.3 %psum.7 = f32[4,768]{1,0:T(4,128)S(1)} all-reduce(f32[4,768]{1,0:T(4,128)S(1)} %pad_maximum_fusion.6), channel_id=1, replica_groups=mesh['dp'=4,'row'=4,'col'=2] {'dp','row','col'}, use_global_device_ids=true, to_apply=%region_12.13 | all-reduce | flops 3072 | bytes 24576 | tf_op jit(solution)/shard_map/psum | solution.py:278
  266.6 5.8 %collective-permute-done = bf16[1024,192]{0,1:T(8,128)(2,1)S(1)} collective-permute-done((bf16[1024,192]{0,1:T(8,128)(2,1)S(1)}, bf16[1024,192]{0,1:T(8,128)(2,1)S(1)}, u32[]{:S(2)}, u32[]{:S(2)}) %collective-permute-start) | collective-permute-done | bytes 393248 | tf_op jit(solution)/shard_map/ppermute | solution.py:272
  274.4 7.5 %all_gather.26 = bf16[192,1920]{1,0:T(8,128)(2,1)S(1)} all-gather(bf16[48,1920]{1,0:T(8,128)(2,1)S(1)} %slice.169), channel_id=1, replica_groups=mesh['dp'=4,'row'=4,'col'=2] {'dp'}, dimensions={0}, use_global_device_ids=true | all-gather | bytes 921600 | tf_op jit(solution)/shard_map/all_gather | solution.py:156
  282.0 7.8 %all_gather.27 = bf16[192,1536]{1,0:T(8,128)(2,1)S(1)} all-gather(bf16[48,1536]{1,0:T(8,128)(2,1)S(1)} %slice-done), channel_id=1, replica_groups=mesh['dp'=4,'row'=4,'col'=2] {'dp'}, dimensions={0}, use_global_device_ids=true | all-gather | bytes 737280 | tf_op jit(solution)/shard_map/all_gather | solution.py:156
  289.8 6.8 %all_gather.25 = bf16[192,1152]{1,0:T(8,128)(2,1)S(1)} all-gather(bf16[48,1152]{1,0:T(8,128)(2,1)S(1)} %slice-done.1), channel_id=1, replica_groups=mesh['dp'=4,'row'=4,'col'=2] {'dp'}, dimensions={0}, use_global_device_ids=true | all-gather | bytes 552960 | tf_op jit(solution)/shard_map/all_gather | solution.py:156
  (188 shorter events, 69.5 us)
Async XLA Ops:
  7.2 83.2 %all-gather.3.cloned.1.call-start = ((), (), s32[]{:S(2)}) async-start(), calls=%async_computation.5 | async-start | bytes 7520256 | tf_op jit(solution)/shard_map/all_gather | solution.py:147
  23.7 6.0 %copy-start.37 = (f32[4,192]{1,0:T(4,128)S(1)}, f32[4,192]{1,0:T(4,128)}, u32[]{:S(2)}) copy-start(f32[4,192]{1,0:T(4,128)} %param.21) | copy-start | bytes 9220
  23.7 46.3 %copy-start.39 = (s32[4,512]{1,0:T(4,128)S(1)}, s32[4,512]{1,0:T(4,128)}, u32[]{:S(2)}) copy-start(s32[4,512]{1,0:T(4,128)} %param.20) | copy-start | bytes 24580
  23.7 47.4 %copy-start.11 = (bf16[1024,192]{0,1:T(8,128)(2,1)S(1)}, bf16[1024,192]{0,1:T(8,128)(2,1)}, u32[]{:S(2)}) copy-start(bf16[1024,192]{0,1:T(8,128)(2,1)} %param.19) | copy-start | bytes 1179652
  24.7 58.1 %all-to-all-start = ((bf16[4,512,192]{1,2,0:T(8,128)(2,1)}), bf16[4,512,192]{1,2,0:T(8,128)(2,1)S(1)}, u32[]{:S(2)}, u32[]{:S(2)}) async-start(bf16[4,512,192]{1,2,0:T(8,128)(2,1)} %bitcast.147), calls=%async_computation | async-start | bytes 1572864 | tf_op jit(solution)/shard_map/all_to_all | solution.py:195
  71.1 23.7 %copy-start.35 = (f32[768]{0:T(1024)}, f32[768]{0:T(1024)S(1)}, u32[]{:S(2)}) copy-start(f32[768]{0:T(1024)S(1)} %get-tuple-element.150) | copy-start | bytes 9220
  82.8 20.4 %all-to-all-start.2 = ((bf16[4,512,192]{1,2,0:T(8,128)(2,1)}), bf16[4,512,192]{1,2,0:T(8,128)(2,1)}, u32[]{:S(2)}, u32[]{:S(2)}) async-start(bf16[4,512,192]{1,2,0:T(8,128)(2,1)} %bitcast.146), calls=%async_computation.2 | async-start | bytes 1572864 | tf_op jit(solution)/shard_map/all_to_all | solution.py:195
  87.0 186.4 %reduce-scatter.4.cloned.1.call-start = ((), (), s32[]{:S(2)}) async-start(), calls=%async_computation.6 | async-start | bytes 7520256
  89.2 5.6 %copy-start.31 = (f32[512]{0:T(512)}, f32[512]{0:T(512)S(1)}, u32[]{:S(2)}) copy-start(f32[512]{0:T(512)S(1)} %get-tuple-element.197) | copy-start | bytes 6148
  89.2 5.6 %copy-start.33 = (f32[512]{0:T(512)}, f32[512]{0:T(512)S(1)}, u32[]{:S(2)}) copy-start(f32[512]{0:T(512)S(1)} %get-tuple-element.198) | copy-start | bytes 6148
  109.7 7.4 %copy-start.8 = (f32[1,512,6,3,64]{1,4,3,2,0:T(8,128)S(1)}, f32[1,512,6,3,64]{1,4,3,2,0:T(8,128)}, u32[]{:S(2)}) copy-start(f32[1,512,6,3,64]{1,4,3,2,0:T(8,128)} %copy-done.7) | copy-start | bytes 7077892
  117.2 4.6 %copy-start = (f32[6,512,512]{1,2,0:T(8,128)S(1)}, f32[6,512,512]{1,2,0:T(8,128)}, u32[]{:S(2)}) copy-start(f32[6,512,512]{1,2,0:T(8,128)} %fusion.1) | copy-start | bytes 18874372
  172.4 20.6 %all-to-all-start.3 = ((bf16[4,512,192]{1,2,0:T(8,128)(2,1)}), bf16[4,512,192]{1,2,0:T(8,128)(2,1)S(1)}, u32[]{:S(2)}, u32[]{:S(2)}) async-start(bf16[4,512,192]{1,2,0:T(8,128)(2,1)} %bitcast.47), calls=%async_computation.3 | async-start | bytes 1572864 | tf_op jit(solution)/shard_map/all_to_all | solution.py:265
  193.0 65.7 %all-to-all-start.1 = ((bf16[4,512,192]{1,2,0:T(8,128)(2,1)}), bf16[4,512,192]{1,2,0:T(8,128)(2,1)S(1)}, u32[]{:S(2)}, u32[]{:S(2)}) async-start(bf16[4,512,192]{1,2,0:T(8,128)(2,1)} %bitcast.29), calls=%async_computation.1 | async-start | bytes 1572864 | tf_op jit(solution)/shard_map/all_to_all | solution.py:265
  199.5 65.1 %collective-permute-start.1 = (bf16[1024,192]{0,1:T(8,128)(2,1)S(1)}, bf16[1024,192]{0,1:T(8,128)(2,1)}, u32[]{:S(2)}, u32[]{:S(2)}) collective-permute-start(bf16[1024,192]{0,1:T(8,128)(2,1)S(1)} %bitcast.162), channel_id=1, source_target_pairs={{0,1},{1,0},{2,3},{3,2},{4,5},{5,4},{6,7},{7,6},{8,9},{9,8},{10,11... | collective-permute-start | bytes 1179656 | tf_op jit(solution)/shard_map/ppermute | solution.py:272
  259.9 4.0 %copy-start.38 = (f32[4,192]{1,0:T(4,128)S(1)}, f32[4,192]{1,0:T(4,128)}, u32[]{:S(2)}) copy-start(f32[4,192]{1,0:T(4,128)} %param.21) | copy-start | bytes 9220
  259.9 4.7 %copy-start.12 = (bf16[1024,192]{0,1:T(8,128)(2,1)S(1)}, bf16[1024,192]{0,1:T(8,128)(2,1)}, u32[]{:S(2)}) copy-start(bf16[1024,192]{0,1:T(8,128)(2,1)} %param.19) | copy-start | bytes 1179652
  261.4 11.1 %copy-start.14 = (bf16[1024,192]{0,1:T(8,128)(2,1)S(1)}, bf16[1024,192]{0,1:T(8,128)(2,1)}, u32[]{:S(2)}) copy-start(bf16[1024,192]{0,1:T(8,128)(2,1)} %param.18) | copy-start | bytes 1179652
  261.5 10.9 %collective-permute-start = (bf16[1024,192]{0,1:T(8,128)(2,1)S(1)}, bf16[1024,192]{0,1:T(8,128)(2,1)S(1)}, u32[]{:S(2)}, u32[]{:S(2)}) collective-permute-start(bf16[1024,192]{0,1:T(8,128)(2,1)S(1)} %bitcast.163), channel_id=1, source_target_pairs={{0,1},{1,0},{2,3},{3,2},{4,5},{5,4},{6,7},{7,6},{8,9},{9,8},{10,11... | collective-permute-start | bytes 1179656 | tf_op jit(solution)/shard_map/ppermute | solution.py:272
  274.4 7.6 %slice-start = ((bf16[48,4608]{1,0:T(8,128)(2,1)}), bf16[48,1536]{1,0:T(8,128)(2,1)S(1)}, s32[]{:S(2)}) async-start(bf16[48,4608]{1,0:T(8,128)(2,1)} %reduce-scatter.4.cloned.1.call-done), calls=%async_computation.7 | async-start | bytes 294912 | tf_op jit(solution)/shard_map/slice | solution.py:155
  274.4 15.4 %slice-start.1 = ((bf16[48,4608]{1,0:T(8,128)(2,1)}), bf16[48,1152]{1,0:T(8,128)(2,1)S(1)}, s32[]{:S(2)}) async-start(bf16[48,4608]{1,0:T(8,128)(2,1)} %reduce-scatter.4.cloned.1.call-done), calls=%async_computation.8 | async-start | bytes 221184 | tf_op jit(solution)/shard_map/slice | solution.py:155
  281.9 14.7 %copy-start.4 = (f32[1536,192]{0,1:T(8,128)S(1)}, f32[1536,192]{0,1:T(8,128)}, u32[]{:S(2)}) copy-start(f32[1536,192]{0,1:T(8,128)} %param.25) | copy-start | bytes 3538948
  281.9 14.7 %copy-start.15 = (f32[1536,192]{0,1:T(8,128)S(1)}, f32[1536,192]{0,1:T(8,128)}, u32[]{:S(2)}) copy-start(f32[1536,192]{0,1:T(8,128)} %param.34) | copy-start | bytes 3538948
  281.9 14.7 %copy-start.16 = (f32[1536,192]{0,1:T(8,128)S(1)}, f32[1536,192]{0,1:T(8,128)}, u32[]{:S(2)}) copy-start(f32[1536,192]{0,1:T(8,128)} %param.35) | copy-start | bytes 3538948
  (32 other events, 77.7 us)
Sparse Core Ops, SparseCore 0:
  10.9 76.4 all-gather.2
  162.7 102.5 reduce-scatter.3
where the time goes:
time: 317 us; the launch traced here: 313 us
  blocking collectives  141 us (44%)
  matrix products  47.2 us (15%)
  local copies, waits for them, and re-layouts  42.3 us (13%)
  other arithmetic  25.5 us (8%)
  waiting for transfers between devices  21.4 us (7%)
  starting transfers between devices  21 us (7%)
  between operations  15 us (5%)
    psum x1, blocking collectives, on_device(): lax.psum(norm_part, ('dp', 'row', 'col'))  57.3 us
    all_gather x1, blocking collectives, on_device(): norm_full = lax.all_gather(norm_params, 'row', axis=1, tiled=True)  40.2 us
    all_gather x3, blocking collectives, reduce_weights(): lax.all_gather(piece, 'dp', axis=0, tiled=True).astype(jnp.float32)  22.1 us
    unnamed x96, local copies, waits for them, and re-layouts  21 us
    all_gather x1, blocking collectives, on_device(): x16 = to_tokens(lax.all_gather(tokens_in, 'col', axis=0, tiled=True))  12.8 us
    dot_general x3, matrix products, dot32(): return jnp.dot(left, right, preferred_element_type=jnp.float32)  12.5 us
    all_to_all x2, waiting for transfers between devices, to_features(): blocks = lax.all_to_all(jnp.moveaxis(blocks, 1, 0), 'row', 0, 0, tiled=True)  11.4 us
    dot_general x3, matrix products, dot_cols(): lax.dot_general(left, right, (((1,), (1,)), ((), ())), preferred_element_...  11.3 us
  transfers between devices with their start and end apart: 8, of which 3 were waited for; matrix products, arithmetic and copies ran while one was open for 12% of the time, Pallas kernels for 0%

commit v1 on v0

--- a/solution.py
+++ b/solution.py
@@ -21,6 +21,17 @@
 inv_sqrt_two_pi = 0.3989422804014327
 
 
+def collect(value, axis, dim):
+    ways = lax.axis_size(axis)
+    pieces = [value]
+    for far in range(1, ways):
+        pieces.append(
+            lax.ppermute(pieces[far - 1], axis, [(d, (d - 1) % ways) for d in range(ways)])
+        )
+    line = jnp.concatenate(pieces, axis=dim)
+    return jnp.roll(line, lax.axis_index(axis) * value.shape[dim], axis=dim)
+
+
 def gelu_value(value):
     return 0.5 * value * (1.0 + lax.erf(value * inv_sqrt_two))
 
@@ -153,7 +164,7 @@
     sums, start = ([], 0)
     for grad in grads:
         piece = part[:, start : start + grad.shape[1]]
-        sums.append(lax.all_gather(piece, "dp", axis=0, tiled=True).astype(jnp.float32))
+        sums.append(collect(piece, "dp", 0).astype(jnp.float32))
         start += grad.shape[1]
     return sums
 

time: 317 us -> 313 us (0.987)
  blocking collectives: 141 us -> 119 us
  starting transfers between devices: 21 us -> 31.1 us
    all_gather x3 -> x0, blocking collectives: 22.1 us -> none  [reduce_weights(): lax.all_gather(piece, 'dp', axis=0, tiled=True).astype(jnp.float32)]
    ppermute x0 -> x9, starting transfers between devices: none -> 10.2 us  [collect(): lax.ppermute(pieces[far - 1], axis, [(d, (d - 1) % ways) for d in range(w...]
    unnamed x96 -> x116, local copies, waits for them, and re-layouts: 21 us -> 21.8 us
  transfers between devices with their start and end apart: 8 -> 17, of which waited for: 3 -> 7; matrix products, arithmetic and copies ran while one was open for 12% -> 15% of each run, Pallas kernels for 0% -> 0%
where the time goes in v1:
time: 313 us; the launch traced here: 308 us
  blocking collectives  119 us (38%)
  matrix products  47.5 us (15%)
  local copies, waits for them, and re-layouts  45.1 us (14%)
  starting transfers between devices  31.1 us (10%)
  other arithmetic  25.6 us (8%)
  waiting for transfers between devices  24.5 us (8%)
  between operations  15.2 us (5%)
    psum x1, blocking collectives, on_device(): lax.psum(norm_part, ('dp', 'row', 'col'))  57.2 us
    all_gather x1, blocking collectives, on_device(): norm_full = lax.all_gather(norm_params, 'row', axis=1, tiled=True)  40.2 us
    unnamed x116, local copies, waits for them, and re-layouts  21.8 us
    dot_general x3, matrix products, dot32(): return jnp.dot(left, right, preferred_element_type=jnp.float32)  12.8 us
    all_gather x1, blocking collectives, on_device(): x16 = to_tokens(lax.all_gather(tokens_in, 'col', axis=0, tiled=True))  12.8 us
    all_to_all x2, waiting for transfers between devices, to_features(): blocks = lax.all_to_all(jnp.moveaxis(blocks, 1, 0), 'row', 0, 0, tiled=True)  11.4 us
    dot_general x3, matrix products, dot_cols(): lax.dot_general(left, right, (((1,), (1,)), ((), ())), preferred_element_...  11.3 us
    ppermute x9, starting transfers between devices, collect(): lax.ppermute(pieces[far - 1], axis, [(d, (d - 1) % ways) for d in range(w...  10.2 us
  transfers between devices with their start and end apart: 17, of which 7 were waited for; matrix products, arithmetic and copies ran while one was open for 15% of the time, Pallas kernels for 0%

profile of v1, /device:TPU:0, one launch (start us, length us, event | category | flops | bytes accessed | tf_op | source)
XLA Modules:
  0.0 307.6 jit_solution(5688831458922785222)
XLA Ops:
  10.9 12.8 %all_gather.12 = bf16[2048,192]{0,1:T(8,128)(2,1)S(1)} all-gather(bf16[1024,192]{0,1:T(8,128)(2,1)S(1)} %copy-done.14), channel_id=1, replica_groups=mesh['dp'=4,'row'=4,'col'=2] {'col'}, dimensions={0}, use_global_device_ids=true | all-gather | bytes 1179648 | tf_op jit(solution)/shard_map/all_gather | solution.py:209
  24.7 5.1 %all-to-all-start = ((bf16[4,512,192]{1,2,0:T(8,128)(2,1)}), bf16[4,512,192]{1,2,0:T(8,128)(2,1)S(1)}, u32[]{:S(2)}, u32[]{:S(2)}) async-start(bf16[4,512,192]{1,2,0:T(8,128)(2,1)} %bitcast.147), calls=%async_computation | async-start | bytes 1572864 | tf_op jit(solution)/shard_map/all_to_all | solution.py:206
  29.8 40.2 %all-gather = f32[4,192,4]{1,2,0:T(4,128)S(1)} all-gather(f32[1,192,4]{1,2,0:T(4,128)S(1)} %bitcast.167), channel_id=1, replica_groups=mesh['dp'=4,'row'=4,'col'=2] {'row'}, dimensions={0}, use_global_device_ids=true | all-gather | bytes 15360 | tf_op jit(solution)/shard_map/all_gather | solution.py:211
  71.1 8.4 %all_gather.15 = bf16[2048,192]{0,1:T(8,128)(2,1)S(1)} all-gather(bf16[1024,192]{0,1:T(8,128)(2,1)S(1)} %copy-done.12), channel_id=1, replica_groups=mesh['dp'=4,'row'=4,'col'=2] {'col'}, dimensions={0}, use_global_device_ids=true | all-gather | bytes 1179648 | tf_op jit(solution)/shard_map/all_gather | solution.py:210
  82.8 4.2 %all-to-all-start.2 = ((bf16[4,512,192]{1,2,0:T(8,128)(2,1)}), bf16[4,512,192]{1,2,0:T(8,128)(2,1)}, u32[]{:S(2)}, u32[]{:S(2)}) async-start(bf16[4,512,192]{1,2,0:T(8,128)(2,1)} %bitcast.146), calls=%async_computation.2 | async-start | bytes 1572864 | tf_op jit(solution)/shard_map/all_to_all | solution.py:206
  94.7 2.7 convolution_bitcast_fusion.1
  98.9 4.3 %all-to-all-done.2 = bf16[4,512,192]{1,2,0:T(8,128)(2,1)} async-done(((bf16[4,512,192]{1,2,0:T(8,128)(2,1)}), bf16[4,512,192]{1,2,0:T(8,128)(2,1)}, u32[]{:S(2)}, u32[]{:S(2)}) %all-to-all-start.2) | async-done | bytes 786464 | tf_op jit(solution)/shard_map/all_to_all | solution.py:206
  103.2 3.9 %convolution_bitcast_fusion = f32[512,1920]{1,0:T(8,128)S(1)} fusion(bf16[512,768]{0,1:T(8,128)(2,1)} %bitcast.31, bf16[768,4608]{1,0:T(8,128)(2,1)} %all-gather.3.cloned.1.call-done), kind=kOutput, calls=%fused_computation.12 | convolution fusion | flops 1509949440 | bytes 7667712 | tf_op jit(solution)/shard_map/dot_general | solution.py:129
  109.7 7.4 %fusion.1 = f32[6,512,512]{1,2,0:T(8,128)} fusion(pred[512,512]{0,1:T(8,128)(4,1)} %fusion.38, bf16[512,6,48]{0,2,1:T(8,128)(2,1)S(1)} %get-tuple-element.230, bf16[512,6,8]{0,2,1:T(8,128)(2,1)S(1)} %get-tuple-element.221, bf16[512,6,8]{0,2,1:T(8,128)(2,1)S(1)} %get-tuple-element.222, bf16[512,6,48]{0,2,1:T(8,128)(2,1)S(1)} %get-tuple-element.229, ...), kind=kOutput, calls=%fused_computation.3 | convolution fusion | flops 415239680 | bytes 7340032 | tf_op jit(solution)/shard_map/while/body/eval_jaxpr/reduce_sum | solution.py:106
  117.2 4.3 %multiply_reduce_fusion.4 = (f32[512,6]{0,1:T(8,128)S(1)}, bf16[6,64,512]{2,1,0:T(8,128)(2,1)}) fusion(bf16[512,6,64]{0,2,1:T(8,128)(2,1)S(1)} %bitcast.152, f32[6,512,512]{1,2,0:T(8,128)} %fusion.1, f32[1,512,6,3,64]{1,4,3,2,0:T(8,128)S(1)} %copy-done.8), kind=kOutput, calls=%fused_computation.92 | convolution fusion | flops 203879424 | bytes 7483392 | tf_op jit(solution)/shard_map/while/body/eval_jaxpr/hqk,khd->qhd/dot_general | solution.py:109
  132.2 6.3 %fusion.9 = (bf16[512,1536]{1,0:T(8,128)(2,1)S(1)}, bf16[512,1536]{1,0:T(8,128)(2,1)}) fusion(f32[512,1920]{1,0:T(8,128)} %copy-done.31, bf16[768,4608]{1,0:T(8,128)(2,1)} %all-gather.3.cloned.1.call-done, f32[512,768]{1,0:T(8,128)S(1)} %copy-done.2, f32[768]{0:T(1024)S(1)} %copy-done.42, f32[768]{0:T(1024)S(1)} %copy-done.41, f32[512]{0:T(512)S(1)} %copy-done.35, ...), kind=kOutput, calls=%fused_computation.17 | convolution fusion | flops 1220149248 | bytes 10233856 | tf_op jit(solution)/shard_map/dot_general | solution.py:129
  139.7 3.2 %convolution_convert_fusion.1 = bf16[768,1536]{1,0:T(8,128)(2,1)} fusion(bf16[512,1536]{1,0:T(8,128)(2,1)S(1)} %get-tuple-element.197, f32[512,768]{1,0:T(8,128)S(1)} %copy-done.2, f32[768]{0:T(1024)S(1)} %copy-done.42, f32[768]{0:T(1024)S(1)} %copy-done.41, f32[512]{0:T(512)S(1)} %copy-done.35, f32[512]{0:T(512)S(1)} %copy-done.33), kind=kOutput, calls=%fused_computation.10 | convolution fusion | flops 1211105280 | bytes 5515264 | tf_op jit(solution)/shard_map/dot_general | solution.py:133
  142.9 2.8 copy.270
  145.7 3.5 %fusion.13 = bf16[768,1920]{0,1:T(8,128)(2,1)S(1)} fusion(bf16[512,768]{0,1:T(8,128)(2,1)} %bitcast.31, bf16[512,1536]{1,0:T(8,128)(2,1)} %get-tuple-element.198, bf16[512,384]{1,0:T(8,128)(2,1)S(1)} %copy.256), kind=kOutput, calls=%fused_computation.23 | convolution fusion | flops 1515356160 | bytes 5701632 | tf_op jit(solution)/shard_map/dot_general | solution.py:133
  149.2 3.4 %pad_maximum_fusion = bf16[768,4608]{0,1:T(8,128)(2,1)} fusion(bf16[768,1920]{0,1:T(8,128)(2,1)S(1)} %fusion.13, bf16[768,1536]{0,1:T(8,128)(2,1)S(1)} %copy.270, bf16[768,1152]{0,1:T(8,128)(2,1)S(1)} %copy-done.1), kind=kLoop, calls=%fused_computation.1 | loop fusion | flops 21233664 | bytes 14155776 | tf_op jit(solution)/shard_map/concatenate | solution.py:162
  152.7 10.2 %copy.282 = bf16[768,4608]{1,0:T(8,128)(2,1)} copy(bf16[768,4608]{0,1:T(8,128)(2,1)} %pad_maximum_fusion) | data formatting | bytes 14155776
  164.3 3.2 %fusion.17 = f32[512,768]{1,0:T(8,128)S(1)} fusion(bf16[512,1536]{1,0:T(8,128)(2,1)S(1)} %copy-done.46, bf16[768,4608]{1,0:T(8,128)(2,1)} %all-gather.3.cloned.1.call-done), kind=kOutput, calls=%fused_computation.28 | convolution fusion | flops 1207959552 | bytes 5505024 | tf_op jit(solution)/shard_map/dot_general | solution.py:139
  167.5 3.5 %multiply_reduce_fusion.1 = (f32[768]{0:T(1024)S(1)}, f32[512]{0:T(512)S(1)}, f32[768]{0:T(1024)S(1)}, f32[768]{0:T(1024)S(1)}, f32[512]{0:T(512)S(1)}, /*index=5*/f32[768]{0:T(1024)S(1)}, f32[512,768]{1,0:T(8,128)S(1)}) fusion(f32[512,768]{1,0:T(8,128)S(1)} %copy-done.3, f32[512]{0:T(512)S(1)} %copy-done.35, f32[512]{0:T(512)S(1)} %copy-done.33, ...), kind=kOutput, calls=%fused_computation.42 | convolution fusion | flops 911470592 | bytes 7694336 | tf_op jit(solution)/shard_map/dot_general | solution.py:139
  172.6 3.5 %all-to-all-start.3 = ((bf16[4,512,192]{1,2,0:T(8,128)(2,1)}), bf16[4,512,192]{1,2,0:T(8,128)(2,1)S(1)}, u32[]{:S(2)}, u32[]{:S(2)}) async-start(bf16[4,512,192]{1,2,0:T(8,128)(2,1)} %bitcast.47), calls=%async_computation.3 | async-start | bytes 1572864 | tf_op jit(solution)/shard_map/all_to_all | solution.py:276
  176.2 4.5 %fusion.27 = bf16[512,768]{1,0:T(8,128)(2,1)S(1)} fusion(bf16[768,4608]{1,0:T(8,128)(2,1)} %all-gather.3.cloned.1.call-done, bf16[512,1536]{1,0:T(8,128)(2,1)} %get-tuple-element.198, bf16[512,384]{1,0:T(8,128)(2,1)S(1)} %copy.256), kind=kOutput, calls=%fused_computation.57 | convolution fusion | flops 1514274816 | bytes 5701632 | tf_op jit(solution)/shard_map/dot_general | solution.py:139
  181.9 11.4 %all-to-all-done.3 = bf16[4,512,192]{1,2,0:T(8,128)(2,1)S(1)} async-done(((bf16[4,512,192]{1,2,0:T(8,128)(2,1)}), bf16[4,512,192]{1,2,0:T(8,128)(2,1)S(1)}, u32[]{:S(2)}, u32[]{:S(2)}) %all-to-all-start.3) | async-done | bytes 786464 | tf_op jit(solution)/shard_map/all_to_all | solution.py:276
  193.2 3.7 %all-to-all-start.1 = ((bf16[4,512,192]{1,2,0:T(8,128)(2,1)}), bf16[4,512,192]{1,2,0:T(8,128)(2,1)S(1)}, u32[]{:S(2)}, u32[]{:S(2)}) async-start(bf16[4,512,192]{1,2,0:T(8,128)(2,1)} %bitcast.29), calls=%async_computation.1 | async-start | bytes 1572864 | tf_op jit(solution)/shard_map/all_to_all | solution.py:276
  201.7 57.2 %psum.7 = f32[4,768]{1,0:T(4,128)S(1)} all-reduce(f32[4,768]{1,0:T(4,128)S(1)} %pad_maximum_fusion.6), channel_id=1, replica_groups=mesh['dp'=4,'row'=4,'col'=2] {'dp','row','col'}, use_global_device_ids=true, to_apply=%region_12.13 | all-reduce | flops 3072 | bytes 24576 | tf_op jit(solution)/shard_map/psum | solution.py:289
  266.8 5.8 %collective-permute-done = bf16[1024,192]{0,1:T(8,128)(2,1)S(1)} collective-permute-done((bf16[1024,192]{0,1:T(8,128)(2,1)S(1)}, bf16[1024,192]{0,1:T(8,128)(2,1)S(1)}, u32[]{:S(2)}, u32[]{:S(2)}) %collective-permute-start) | collective-permute-done | bytes 393248 | tf_op jit(solution)/shard_map/ppermute | solution.py:283
  (224 shorter events, 76.9 us)
Async XLA Ops:
  7.2 83.2 %all-gather.3.cloned.1.call-start = ((), (), s32[]{:S(2)}) async-start(), calls=%async_computation.5 | async-start | bytes 7520256 | tf_op jit(solution)/shard_map/all_gather | solution.py:158
  23.7 46.3 %copy-start.40 = (s32[4,512]{1,0:T(4,128)S(1)}, s32[4,512]{1,0:T(4,128)}, u32[]{:S(2)}) copy-start(s32[4,512]{1,0:T(4,128)} %param.20) | copy-start | bytes 24580
  23.7 47.4 %copy-start.12 = (bf16[1024,192]{0,1:T(8,128)(2,1)S(1)}, bf16[1024,192]{0,1:T(8,128)(2,1)}, u32[]{:S(2)}) copy-start(bf16[1024,192]{0,1:T(8,128)(2,1)} %param.19) | copy-start | bytes 1179652
  24.7 58.1 %all-to-all-start = ((bf16[4,512,192]{1,2,0:T(8,128)(2,1)}), bf16[4,512,192]{1,2,0:T(8,128)(2,1)S(1)}, u32[]{:S(2)}, u32[]{:S(2)}) async-start(bf16[4,512,192]{1,2,0:T(8,128)(2,1)} %bitcast.147), calls=%async_computation | async-start | bytes 1572864 | tf_op jit(solution)/shard_map/all_to_all | solution.py:206
  71.1 23.6 %copy-start.36 = (f32[768]{0:T(1024)}, f32[768]{0:T(1024)S(1)}, u32[]{:S(2)}) copy-start(f32[768]{0:T(1024)S(1)} %get-tuple-element.172) | copy-start | bytes 9220
  82.8 20.4 %all-to-all-start.2 = ((bf16[4,512,192]{1,2,0:T(8,128)(2,1)}), bf16[4,512,192]{1,2,0:T(8,128)(2,1)}, u32[]{:S(2)}, u32[]{:S(2)}) async-start(bf16[4,512,192]{1,2,0:T(8,128)(2,1)} %bitcast.146), calls=%async_computation.2 | async-start | bytes 1572864 | tf_op jit(solution)/shard_map/all_to_all | solution.py:206
  87.0 186.6 %reduce-scatter.4.cloned.1.call-start = ((), (), s32[]{:S(2)}) async-start(), calls=%async_computation.6 | async-start | bytes 7520256 | tf_op jit(solution)/shard_map/reduce_scatter | solution.py:163
  172.6 20.6 %all-to-all-start.3 = ((bf16[4,512,192]{1,2,0:T(8,128)(2,1)}), bf16[4,512,192]{1,2,0:T(8,128)(2,1)S(1)}, u32[]{:S(2)}, u32[]{:S(2)}) async-start(bf16[4,512,192]{1,2,0:T(8,128)(2,1)} %bitcast.47), calls=%async_computation.3 | async-start | bytes 1572864 | tf_op jit(solution)/shard_map/all_to_all | solution.py:276
  193.2 65.6 %all-to-all-start.1 = ((bf16[4,512,192]{1,2,0:T(8,128)(2,1)}), bf16[4,512,192]{1,2,0:T(8,128)(2,1)S(1)}, u32[]{:S(2)}, u32[]{:S(2)}) async-start(bf16[4,512,192]{1,2,0:T(8,128)(2,1)} %bitcast.29), calls=%async_computation.1 | async-start | bytes 1572864 | tf_op jit(solution)/shard_map/all_to_all | solution.py:276
  199.7 65.0 %collective-permute-start.1 = (bf16[1024,192]{0,1:T(8,128)(2,1)S(1)}, bf16[1024,192]{0,1:T(8,128)(2,1)}, u32[]{:S(2)}, u32[]{:S(2)}) collective-permute-start(bf16[1024,192]{0,1:T(8,128)(2,1)S(1)} %bitcast.162), channel_id=1, source_target_pairs={{0,1},{1,0},{2,3},{3,2},{4,5},{5,4},{6,7},{7,6},{8,9},{9,8},{10,11... | collective-permute-start | bytes 1179656 | tf_op jit(solution)/shard_map/ppermute | solution.py:283
  261.7 10.9 %collective-permute-start = (bf16[1024,192]{0,1:T(8,128)(2,1)S(1)}, bf16[1024,192]{0,1:T(8,128)(2,1)S(1)}, u32[]{:S(2)}, u32[]{:S(2)}) collective-permute-start(bf16[1024,192]{0,1:T(8,128)(2,1)S(1)} %bitcast.163), channel_id=1, source_target_pairs={{0,1},{1,0},{2,3},{3,2},{4,5},{5,4},{6,7},{7,6},{8,9},{9,8},{10,11... | collective-permute-start | bytes 1179656 | tf_op jit(solution)/shard_map/ppermute | solution.py:283
  273.6 13.9 %copy-start.11 = (bf16[48,4608]{1,0:T(8,128)(2,1)S(1)}, bf16[48,4608]{1,0:T(8,128)(2,1)}, u32[]{:S(2)}) copy-start(bf16[48,4608]{1,0:T(8,128)(2,1)} %reduce-scatter.4.cloned.1.call-done) | copy-start | bytes 1327108
  274.6 5.9 %collective-permute-start.8 = (bf16[48,1536]{1,0:T(8,128)(2,1)S(1)}, bf16[48,1536]{1,0:T(8,128)(2,1)S(1)}, u32[]{:S(2)}, u32[]{:S(2)}) collective-permute-start(bf16[48,1536]{1,0:T(8,128)(2,1)S(1)} %get-tuple-element.213), channel_id=1, source_target_pairs={{0,24},{8,0},{16,8},{24,16},{1,25},{9,1},{17,9},{25,17},{2,26},{10... | collective-permute-start | bytes 442376 | tf_op jit(solution)/shard_map/ppermute | solution.py:29
  275.6 12.0 %copy-start.10 = (f32[192,1152]{1,0:T(8,128)S(1)}, f32[192,1152]{1,0:T(8,128)}, u32[]{:S(2)}) copy-start(f32[192,1152]{1,0:T(8,128)} %param.22) | copy-start | bytes 2654212
  275.6 12.0 %copy-start.24 = (f32[192,1152]{1,0:T(8,128)S(1)}, f32[192,1152]{1,0:T(8,128)}, u32[]{:S(2)}) copy-start(f32[192,1152]{1,0:T(8,128)} %param.28) | copy-start | bytes 2654212
  275.6 12.0 %copy-start.25 = (f32[192,1152]{1,0:T(8,128)S(1)}, f32[192,1152]{1,0:T(8,128)}, u32[]{:S(2)}) copy-start(f32[192,1152]{1,0:T(8,128)} %param.29) | copy-start | bytes 2654212
  275.6 3.0 collective-permute-start.2
  277.4 3.3 %collective-permute-start.5 = (bf16[48,1920]{1,0:T(8,128)(2,1)S(1)}, bf16[48,1920]{1,0:T(8,128)(2,1)S(1)}, u32[]{:S(2)}, u32[]{:S(2)}) collective-permute-start(bf16[48,1920]{1,0:T(8,128)(2,1)S(1)} %get-tuple-element.215), channel_id=1, source_target_pairs={{0,24},{8,0},{16,8},{24,16},{1,25},{9,1},{17,9},{25,17},{2,26},{10... | collective-permute-start | bytes 552968 | tf_op jit(solution)/shard_map/ppermute | solution.py:29
  278.7 4.2 %collective-permute-start.3 = (bf16[48,1152]{1,0:T(8,128)(2,1)S(1)}, bf16[48,1152]{1,0:T(8,128)(2,1)S(1)}, u32[]{:S(2)}, u32[]{:S(2)}) collective-permute-start(bf16[48,1152]{1,0:T(8,128)(2,1)S(1)} %collective-permute-done.2), channel_id=1, source_target_pairs={{0,24},{8,0},{16,8},{24,16},{1,25},{9,1},{17,9},{25,17},{2,26},{10... | collective-permute-start | bytes 331784 | tf_op jit(solution)/shard_map/ppermute | solution.py:29
  280.6 4.2 %collective-permute-start.9 = (bf16[48,1536]{1,0:T(8,128)(2,1)S(1)}, bf16[48,1536]{1,0:T(8,128)(2,1)S(1)}, u32[]{:S(2)}, u32[]{:S(2)}) collective-permute-start(bf16[48,1536]{1,0:T(8,128)(2,1)S(1)} %collective-permute-done.8), channel_id=1, source_target_pairs={{0,24},{8,0},{16,8},{24,16},{1,25},{9,1},{17,9},{25,17},{2,26},{10... | collective-permute-start | bytes 442376 | tf_op jit(solution)/shard_map/ppermute | solution.py:29
  280.7 9.0 %collective-permute-start.6 = (bf16[48,1920]{1,0:T(8,128)(2,1)S(1)}, bf16[48,1920]{1,0:T(8,128)(2,1)S(1)}, u32[]{:S(2)}, u32[]{:S(2)}) collective-permute-start(bf16[48,1920]{1,0:T(8,128)(2,1)S(1)} %collective-permute-done.5), channel_id=1, source_target_pairs={{0,24},{8,0},{16,8},{24,16},{1,25},{9,1},{17,9},{25,17},{2,26},{10... | collective-permute-start | bytes 552968 | tf_op jit(solution)/shard_map/ppermute | solution.py:29
  282.9 4.7 %collective-permute-start.4 = (bf16[48,1152]{1,0:T(8,128)(2,1)S(1)}, bf16[48,1152]{1,0:T(8,128)(2,1)S(1)}, u32[]{:S(2)}, u32[]{:S(2)}) collective-permute-start(bf16[48,1152]{1,0:T(8,128)(2,1)S(1)} %collective-permute-done.3), channel_id=1, source_target_pairs={{0,24},{8,0},{16,8},{24,16},{1,25},{9,1},{17,9},{25,17},{2,26},{10... | collective-permute-start | bytes 331784 | tf_op jit(solution)/shard_map/ppermute | solution.py:29
  284.7 7.1 %collective-permute-start.10 = (bf16[48,1536]{1,0:T(8,128)(2,1)S(1)}, bf16[48,1536]{1,0:T(8,128)(2,1)S(1)}, u32[]{:S(2)}, u32[]{:S(2)}) collective-permute-start(bf16[48,1536]{1,0:T(8,128)(2,1)S(1)} %collective-permute-done.9), channel_id=1, source_target_pairs={{0,24},{8,0},{16,8},{24,16},{1,25},{9,1},{17,9},{25,17},{2,26},{10... | collective-permute-start | bytes 442376 | tf_op jit(solution)/shard_map/ppermute | solution.py:29
  289.7 5.2 %collective-permute-start.7 = (bf16[48,1920]{1,0:T(8,128)(2,1)S(1)}, bf16[48,1920]{1,0:T(8,128)(2,1)S(1)}, u32[]{:S(2)}, u32[]{:S(2)}) collective-permute-start(bf16[48,1920]{1,0:T(8,128)(2,1)S(1)} %collective-permute-done.6), channel_id=1, source_target_pairs={{0,24},{8,0},{16,8},{24,16},{1,25},{9,1},{17,9},{25,17},{2,26},{10... | collective-permute-start | bytes 552968 | tf_op jit(solution)/shard_map/ppermute | solution.py:29
  (40 other events, 126.7 us)
Sparse Core Ops, SparseCore 0:
  10.9 76.4 all-gather.2
  163.0 102.5 reduce-scatter.3
